TPU v7x, 32 devices: a whole 2x2x4 slice. The times are simulated.
32 devices in a mesh: dp: 4 (over y, x), tensor: 8 (over z, core).
Axes of the slice: x: 2, y: 2, z: 4, core: 2. Of those that a mesh axis runs over, the one named last changes fastest.
Arguments:
- inputs: bfloat16 [16384, 2048], P(('dp', 'tensor')), may hold values from -6 to 6
- block_ids: int32 [16, 1024], P('dp'), may hold values from 0 to 4, never falling along the last dimension, each value on 1 to 256 neighbouring positions
- norm_gain: bfloat16 [2048], replicated, may hold values from 0.5 to 1.5
- norm_bias: bfloat16 [2048], replicated, may hold values from -3 to 3
- query_weight: bfloat16 [2048, 2048], P('dp', 'tensor'), may hold values from -0.125 to 0.125
- query_bias: bfloat16 [2048], P('tensor'), may hold values from -3 to 3
- key_weight: bfloat16 [2048, 2048], P('dp', 'tensor'), may hold values from -0.125 to 0.125
- key_bias: bfloat16 [2048], P('tensor'), may hold values from -3 to 3
- value_weight: bfloat16 [2048, 2048], P('dp', 'tensor'), may hold values from -0.125 to 0.125
- value_bias: bfloat16 [2048], P('tensor'), may hold values from -3 to 3
- out_weight: bfloat16 [2048, 2048], P('tensor', 'dp'), may hold values from -3 to 3
- out_bias: bfloat16 [2048], replicated, may hold values from -3 to 3
- up_weight: bfloat16 [2048, 8192], P('dp', 'tensor'), may hold values from -0.125 to 0.125
- up_bias: bfloat16 [8192], P('tensor'), may hold values from -3 to 3
- down_weight: bfloat16 [8192, 2048], P('tensor', 'dp'), may hold values from -0.09375 to 0.09375
- down_bias: bfloat16 [2048], replicated, may hold values from -3 to 3
- grad_out: bfloat16 [16384, 2048], P(('dp', 'tensor')), may hold values from -6 to 6
Outputs:
- output: bfloat16 [16384, 2048], P(('dp', 'tensor'))
- input_grad: bfloat16 [16384, 2048], P(('dp', 'tensor'))
- norm_gain_grad: float32 [2048], replicated
- norm_bias_grad: float32 [2048], replicated
- query_weight_grad: float32 [2048, 2048], P('dp', 'tensor')
- query_bias_grad: float32 [2048], P('tensor')
- key_weight_grad: float32 [2048, 2048], P('dp', 'tensor')
- key_bias_grad: float32 [2048], P('tensor')
- value_weight_grad: float32 [2048, 2048], P('dp', 'tensor')
- value_bias_grad: float32 [2048], P('tensor')
- out_weight_grad: float32 [2048, 2048], P('tensor', 'dp')
- out_bias_grad: float32 [2048], replicated
- up_weight_grad: float32 [2048, 8192], P('dp', 'tensor')
- up_bias_grad: float32 [8192], P('tensor')
- down_weight_grad: float32 [8192, 2048], P('tensor', 'dp')
- down_bias_grad: float32 [2048], replicated
Inputs may be any that keep to these rules, and one draw needn't show every extreme that they name: `block_ids`: in each sequence the block numbers never fall along the positions; a block spans 1 to 256 positions, and one block of each sequence spans exactly 256.
All inputs are finite; a program needn't handle non-finite values.
Results may differ from a plain program's by a relative error of at most 0.012.
The roundings to bfloat16 on the way count: a program that leaves them out, or rounds other values in their place, can miss the bound.
Values may be sent and summed in bfloat16 or wider, within the bound.
A program may use at most 320 MiB of HBM per device.

v0:
```python
import jax
import jax.numpy as jnp
from jax import lax
from jax.sharding import PartitionSpec as P

HEAD_DIM = 64
ROT = 32
eps_norm = 1e-05


def normalize(values, gain_in, shift_in):
    center = jnp.mean(values, axis=-1, keepdims=True)
    centered = values - center
    variance = jnp.mean(centered * centered, axis=-1, keepdims=True)
    return centered * lax.rsqrt(variance + eps_norm) * gain_in + shift_in


def rotary_tables(length, rot_width):
    halves = rot_width // 2
    exponent = jnp.arange(halves, dtype=jnp.float32) * (2.0 / rot_width)
    frequency = jnp.power(10000.0, -exponent)
    angles = jnp.arange(length, dtype=jnp.float32)[:, None] * frequency[None, :]
    angles = jnp.concatenate([angles, angles], axis=1)
    return (jnp.cos(angles), jnp.sin(angles))


def rotate(per_head, cos_table, sin_table):
    rot_width = cos_table.shape[-1]
    halves = rot_width // 2
    first_half = per_head[..., :halves]
    second_half = per_head[..., halves:rot_width]
    turned = jnp.concatenate([-second_half, first_half], axis=-1)
    rotated = per_head[..., :rot_width] * cos_table[:, None, :] + turned * sin_table[:, None, :]
    return jnp.concatenate([rotated, per_head[..., rot_width:]], axis=-1)


def masked_scores(query_block, key_block, query_ids, key_ids):
    raw_scores = jnp.einsum(
        "qhd,khd->hqk", query_block, key_block, preferred_element_type=jnp.float32
    ) * HEAD_DIM ** (-0.5)
    allowed = key_ids[None, None, :] <= query_ids[None, :, None]
    return jnp.where(allowed, raw_scores, -1000000000.0)


def gelu_tanh(values):
    return jax.nn.gelu(values, approximate=True)


def per_device(
    inputs,
    block_ids,
    norm_gain,
    norm_bias,
    query_weight,
    query_bias,
    key_weight,
    key_bias,
    value_weight,
    value_bias,
    out_weight,
    out_bias,
    up_weight,
    up_bias,
    down_weight,
    down_bias,
    grad_out,
):
    seq_count, length = block_ids.shape
    local_width = query_weight.shape[1]
    local_heads = local_width // HEAD_DIM
    block_rows = min(512, length)
    per_sequence = length // block_rows
    all_rows = seq_count * length
    score_scale = HEAD_DIM ** (-0.5)
    gain_float = norm_gain.astype(jnp.float32)
    shift_float = norm_bias.astype(jnp.float32)
    inputs_float = inputs.astype(jnp.float32)
    normed = normalize(inputs_float, gain_float, shift_float).astype(jnp.bfloat16)
    full_query, full_key, full_value, full_up, full_out, full_down = (
        lax.all_gather(query_weight, "dp", axis=0, tiled=True),
        lax.all_gather(key_weight, "dp", axis=0, tiled=True),
        lax.all_gather(value_weight, "dp", axis=0, tiled=True),
        lax.all_gather(up_weight, "dp", axis=0, tiled=True),
        lax.all_gather(out_weight, "dp", axis=1, tiled=True),
        lax.all_gather(down_weight, "dp", axis=1, tiled=True),
    )
    group_rows = lax.all_gather(normed, "tensor", axis=0, tiled=True)
    cos_table, sin_table = rotary_tables(length, ROT)

    def project(weight_part, bias_part):
        return jnp.dot(
            group_rows, weight_part, preferred_element_type=jnp.float32
        ) + bias_part.astype(jnp.float32)

    def split_heads(values):
        return values.reshape(seq_count, length, local_heads, HEAD_DIM)

    queries = rotate(split_heads(project(full_query, query_bias)), cos_table, sin_table).astype(
        jnp.bfloat16
    )
    key_rows = rotate(split_heads(project(full_key, key_bias)), cos_table, sin_table).astype(
        jnp.bfloat16
    )
    value_rows = split_heads(project(full_value, value_bias)).astype(jnp.bfloat16)

    def forward_block(block_index):
        sequence = block_index // per_sequence
        offset = block_index % per_sequence * block_rows
        seq_ids = block_ids[sequence]
        query_block = lax.dynamic_slice_in_dim(queries[sequence], offset, block_rows, 0)
        query_ids = lax.dynamic_slice_in_dim(seq_ids, offset, block_rows, 0)
        scores = masked_scores(query_block, key_rows[sequence], query_ids, seq_ids)
        highest = jnp.max(scores, axis=2, keepdims=True)
        shifted = jnp.exp(scores - highest)
        totals = jnp.sum(shifted, axis=2, keepdims=True)
        weights_low = (shifted / totals).astype(jnp.bfloat16)
        mixed_rows = jnp.einsum(
            "hqk,khd->qhd", weights_low, value_rows[sequence], preferred_element_type=jnp.float32
        )
        return (mixed_rows, (highest + jnp.log(totals))[:, :, 0])

    attended, log_sums = lax.map(forward_block, jnp.arange(seq_count * per_sequence))
    attended_low = attended.reshape(all_rows, local_width).astype(jnp.bfloat16)
    hidden = project(full_up, up_bias)
    active = gelu_tanh(hidden).astype(jnp.bfloat16)
    branch_rows = lax.psum_scatter(
        jnp.dot(attended_low, full_out, preferred_element_type=jnp.float32)
        + jnp.dot(active, full_down, preferred_element_type=jnp.float32),
        "tensor",
        scatter_dimension=0,
        tiled=True,
    )
    output = (
        inputs_float + branch_rows + out_bias.astype(jnp.float32) + down_bias.astype(jnp.float32)
    ).astype(jnp.bfloat16)
    back_query, back_key, back_value, back_up, back_out, back_down = (
        lax.all_gather(query_weight, "dp", axis=0, tiled=True),
        lax.all_gather(key_weight, "dp", axis=0, tiled=True),
        lax.all_gather(value_weight, "dp", axis=0, tiled=True),
        lax.all_gather(up_weight, "dp", axis=0, tiled=True),
        lax.all_gather(out_weight, "dp", axis=1, tiled=True),
        lax.all_gather(down_weight, "dp", axis=1, tiled=True),
    )
    back_rows = lax.all_gather(normed, "tensor", axis=0, tiled=True)
    upstream = lax.all_gather(grad_out, "tensor", axis=0, tiled=True)
    out_wgrad = jnp.einsum("rk,rd->kd", attended_low, upstream, preferred_element_type=jnp.float32)
    down_wgrad = jnp.einsum("rf,rd->fd", active, upstream, preferred_element_type=jnp.float32)
    attended_grad = jnp.einsum(
        "rd,kd->rk", upstream, back_out, preferred_element_type=jnp.float32
    ).astype(jnp.bfloat16)
    active_grad = jnp.einsum("rd,fd->rf", upstream, back_down, preferred_element_type=jnp.float32)
    unused_value, gelu_pull = jax.vjp(gelu_tanh, hidden)
    hidden_grad = gelu_pull(active_grad)[0].astype(jnp.bfloat16)
    grad_heads = split_heads(attended_grad)
    sums_grouped = log_sums.reshape(seq_count, per_sequence, local_heads, block_rows)

    def backward_sequence(sequence):
        seq_ids = block_ids[sequence]
        seq_queries = queries[sequence]
        seq_keys = key_rows[sequence]
        seq_values = value_rows[sequence]
        seq_grads = grad_heads[sequence]
        seq_sums = sums_grouped[sequence]

        def backward_block(running, block_number):
            key_total, value_total = running
            offset = block_number * block_rows
            query_block = lax.dynamic_slice_in_dim(seq_queries, offset, block_rows, 0)
            query_ids = lax.dynamic_slice_in_dim(seq_ids, offset, block_rows, 0)
            grad_block = lax.dynamic_slice_in_dim(seq_grads, offset, block_rows, 0)
            scores = masked_scores(query_block, seq_keys, query_ids, seq_ids)
            prob_rows = jnp.exp(scores - seq_sums[block_number][:, :, None])
            value_total = value_total + jnp.einsum(
                "hqk,qhd->khd",
                prob_rows.astype(jnp.bfloat16),
                grad_block,
                preferred_element_type=jnp.float32,
            )
            prob_grad = jnp.einsum(
                "qhd,khd->hqk", grad_block, seq_values, preferred_element_type=jnp.float32
            )
            row_inner = jnp.sum(prob_grad * prob_rows, axis=2, keepdims=True)
            score_grad = (prob_rows * (prob_grad - row_inner)).astype(jnp.bfloat16)
            query_part = (
                jnp.einsum("hqk,khd->qhd", score_grad, seq_keys, preferred_element_type=jnp.float32)
                * score_scale
            )
            key_total = (
                key_total
                + jnp.einsum(
                    "hqk,qhd->khd", score_grad, query_block, preferred_element_type=jnp.float32
                )
                * score_scale
            )
            return ((key_total, value_total), query_part)

        zero_total = jnp.zeros((length, local_heads, HEAD_DIM), jnp.float32)
        (key_total, value_total), query_parts = lax.scan(
            backward_block, (zero_total, zero_total), jnp.arange(per_sequence)
        )
        return (query_parts.reshape(length, local_heads, HEAD_DIM), key_total, value_total)

    query_grad_rot, key_grad_rot, value_grad_all = lax.map(backward_sequence, jnp.arange(seq_count))
    query_grad = (
        rotate(query_grad_rot, cos_table, -sin_table)
        .reshape(all_rows, local_width)
        .astype(jnp.bfloat16)
    )
    key_grad = (
        rotate(key_grad_rot, cos_table, -sin_table)
        .reshape(all_rows, local_width)
        .astype(jnp.bfloat16)
    )
    value_grad = value_grad_all.reshape(all_rows, local_width).astype(jnp.bfloat16)
    query_wgrad = jnp.einsum("rd,rk->dk", back_rows, query_grad, preferred_element_type=jnp.float32)
    key_wgrad = jnp.einsum("rd,rk->dk", back_rows, key_grad, preferred_element_type=jnp.float32)
    value_wgrad = jnp.einsum("rd,rk->dk", back_rows, value_grad, preferred_element_type=jnp.float32)
    up_wgrad = jnp.einsum("rd,rf->df", back_rows, hidden_grad, preferred_element_type=jnp.float32)
    normed_grad = lax.psum_scatter(
        jnp.einsum("rk,dk->rd", query_grad, back_query, preferred_element_type=jnp.float32)
        + jnp.einsum("rk,dk->rd", key_grad, back_key, preferred_element_type=jnp.float32)
        + jnp.einsum("rk,dk->rd", value_grad, back_value, preferred_element_type=jnp.float32)
        + jnp.einsum("rf,df->rd", hidden_grad, back_up, preferred_element_type=jnp.float32),
        "tensor",
        scatter_dimension=0,
        tiled=True,
    )
    unused_norm, norm_pull = jax.vjp(normalize, inputs_float, gain_float, shift_float)
    input_part, gain_part, shift_part = norm_pull(normed_grad)
    input_grad = (grad_out.astype(jnp.float32) + input_part).astype(jnp.bfloat16)
    bias_part = jnp.sum(grad_out, axis=0, dtype=jnp.float32)
    gain_grad, shift_grad, outer_bias_grad = lax.psum(
        (gain_part, shift_part, bias_part), ("dp", "tensor")
    )
    query_bias_grad, key_bias_grad, value_bias_grad, up_bias_grad = lax.psum(
        (
            jnp.sum(query_grad, axis=0, dtype=jnp.float32),
            jnp.sum(key_grad, axis=0, dtype=jnp.float32),
            jnp.sum(value_grad, axis=0, dtype=jnp.float32),
            jnp.sum(hidden_grad, axis=0, dtype=jnp.float32),
        ),
        "dp",
    )
    (
        query_weight_grad,
        key_weight_grad,
        value_weight_grad,
        up_weight_grad,
        out_weight_grad,
        down_weight_grad,
    ) = (
        lax.psum_scatter(query_wgrad, "dp", scatter_dimension=0, tiled=True),
        lax.psum_scatter(key_wgrad, "dp", scatter_dimension=0, tiled=True),
        lax.psum_scatter(value_wgrad, "dp", scatter_dimension=0, tiled=True),
        lax.psum_scatter(up_wgrad, "dp", scatter_dimension=0, tiled=True),
        lax.psum_scatter(out_wgrad, "dp", scatter_dimension=1, tiled=True),
        lax.psum_scatter(down_wgrad, "dp", scatter_dimension=1, tiled=True),
    )
    return (
        output,
        input_grad,
        gain_grad,
        shift_grad,
        query_weight_grad,
        query_bias_grad,
        key_weight_grad,
        key_bias_grad,
        value_weight_grad,
        value_bias_grad,
        out_weight_grad,
        outer_bias_grad,
        up_weight_grad,
        up_bias_grad,
        down_weight_grad,
        outer_bias_grad,
    )


def solution(mesh):
    return jax.shard_map(
        per_device,
        mesh=mesh,
        in_specs=(
            P(("dp", "tensor"), None),
            P("dp", None),
            P(),
            P(),
            P("dp", "tensor"),
            P("tensor"),
            P("dp", "tensor"),
            P("tensor"),
            P("dp", "tensor"),
            P("tensor"),
            P("tensor", "dp"),
            P(),
            P("dp", "tensor"),
            P("tensor"),
            P("tensor", "dp"),
            P(),
            P(("dp", "tensor"), None),
        ),
        out_specs=(
            P(("dp", "tensor"), None),
            P(("dp", "tensor"), None),
            P(),
            P(),
            P("dp", "tensor"),
            P("tensor"),
            P("dp", "tensor"),
            P("tensor"),
            P("dp", "tensor"),
            P("tensor"),
            P("tensor", "dp"),
            P(),
            P("dp", "tensor"),
            P("tensor"),
            P("tensor", "dp"),
            P(),
        ),
        check_vma=False,
    )
```

profile of v0, /device:TPU:0, one launch (start us, length us, event | category | flops | bytes accessed | tf_op | source)
XLA Modules:
  0.0 2073.4 jit_solution(4787446761198307838)
XLA Ops:
  39.2 153.3 %all-gather.9.cloned.1.call-done = bf16[4096,2048]{1,0:T(8,128)(2,1)} async-done(((bf16[512,2048]{1,0:T(8,128)(2,1)}), bf16[4096,2048]{1,0:T(8,128)(2,1)}) %all-gather.9.cloned.1.call-update) | async-done | bytes 16777232 | tf_op jit(solution)/shard_map/all_gather | solution.py:87
  278.6 149.8 %all-gather.23.cloned.1.call-done = bf16[4096,2048]{1,0:T(8,128)(2,1)} async-done(((bf16[512,2048]{1,0:T(8,128)(2,1)}), bf16[4096,2048]{1,0:T(8,128)(2,1)}) %all-gather.23.cloned.1.call-update) | async-done | bytes 16777232 | tf_op jit(solution)/shard_map/all_gather | solution.py:145
  466.2 102.8 %while.44 = (s32[]{:T(128)}, bf16[8,512,4,64]{1,3,2,0:T(8,128)(2,1)S(1)}, f32[8,4,512]{2,1,0:T(4,128)S(1)}, s32[8]{0:T(128)S(1)}, bf16[4,1024,4,64]{1,3,2,0:T(8,...) while((s32[]{:T(128)}, ...), condition=%wide.region_5.6_spmd, body=%wide.region_2.5_spmd.sunk | while | flops 562558976 | bytes 29182452 | solution.py:122
  570.3 342.7 %while.46 = (s32[]{:T(128)}, f32[4,1024,4,64]{1,0,3,2:T(4,128)}, f32[4,1024,4,64]{1,0,3,2:T(4,128)}, bf16[4,1024,4,64]{1,3,2,0:T(8,128)(2,1)}, s32[4]{0:T(128)S(...) while((s32[]{:T(128)}, f32[4,1024,4,64]{1,0,3,2:T(4,128)}, ...), condition=%wide.region_11.12_spmd, body=%wide.region_7.11_spmd.sunk | while | flops 1375598592 | bytes 110209856 | solution.py:203
  575.7 33.3 %while.47 = (s32[]{:T(128)}, f32[1024,4,64]{0,2,1:T(8,128)S(1)}, f32[1024,4,64]{0,2,1:T(8,128)}, f32[2,512,4,64]{1,3,2,0:T(8,128)}, s32[2]{0:T(128)S(1)}, /*inde...) while((s32[]{:T(128)}, f32[1024,4,64]{0,2,1:T(8,128)S(1)}, ...), condition=%wide.region_10.10_spmd.clone, body=%wide.region_8.9_spmd.clone.sunk | while | flops 1375598592 | bytes 89196952 | solution.py:198
  636.1 19.9 dynamic_update_slice.45
  661.3 33.3 %while.47 = (s32[]{:T(128)}, f32[1024,4,64]{0,2,1:T(8,128)S(1)}, f32[1024,4,64]{0,2,1:T(8,128)}, f32[2,512,4,64]{1,3,2,0:T(8,128)}, s32[2]{0:T(128)S(1)}, /*inde...) while((s32[]{:T(128)}, f32[1024,4,64]{0,2,1:T(8,128)S(1)}, ...), condition=%wide.region_10.10_spmd.clone, body=%wide.region_8.9_spmd.clone.sunk | while | flops 1375598592 | bytes 89196952 | solution.py:198
  746.9 33.3 %while.47 = (s32[]{:T(128)}, f32[1024,4,64]{0,2,1:T(8,128)S(1)}, f32[1024,4,64]{0,2,1:T(8,128)}, f32[2,512,4,64]{1,3,2,0:T(8,128)}, s32[2]{0:T(128)S(1)}, /*inde...) while((s32[]{:T(128)}, f32[1024,4,64]{0,2,1:T(8,128)S(1)}, ...), condition=%wide.region_10.10_spmd.clone, body=%wide.region_8.9_spmd.clone.sunk | while | flops 1375598592 | bytes 89196952 | solution.py:198
  832.5 33.3 %while.47 = (s32[]{:T(128)}, f32[1024,4,64]{0,2,1:T(8,128)S(1)}, f32[1024,4,64]{0,2,1:T(8,128)}, f32[2,512,4,64]{1,3,2,0:T(8,128)}, s32[2]{0:T(128)S(1)}, /*inde...) while((s32[]{:T(128)}, f32[1024,4,64]{0,2,1:T(8,128)S(1)}, ...), condition=%wide.region_10.10_spmd.clone, body=%wide.region_8.9_spmd.clone.sunk | while | flops 1375598592 | bytes 89196952 | solution.py:198
  892.9 19.9 dynamic_update_slice.45
  972.8 23.4 %fusion.80 = f32[4096,1024]{1,0:T(8,128)} fusion(bf16[4096,2048]{1,0:T(8,128)(2,1)} %all-gather.9.cloned.1.call-done, bf16[2048,1024]{1,0:T(8,128)(2,1)} %all-gather.19.cloned.1.call-done), kind=kOutput, calls=%fused_computation.136 | convolution fusion | flops 17179869184 | bytes 37748736 | tf_op jit(solution)/shard_map/dot_general | solution.py:91
  996.2 36.5 %convert_reduce_fusion = (f32[1024]{0:T(1024)}, bf16[4096,1024]{1,0:T(8,128)(2,1)}) fusion(f32[4096,1024]{1,0:T(8,128)} %fusion.80, f32[1024]{0:T(1024)S(1)} %copy-done.40, bf16[4096,2048]{1,0:T(8,128)(2,1)} %all-gather.23.cloned.1.call-done, bf16[1024,2048]{1,0:T(8,128)(2,1)} %all-gather.21.cloned.1.call-done), kind=kOutput, calls=%fused_computation.68 | convolution fusion | flops 17276338176 | bytes 46145536 | tf_op jit(solution)/shard_map/rd,fd->rf/dot_general | solution.py:151
  1032.6 48.6 %add_add_fusion = f32[4096,2048]{1,0:T(8,128)} fusion(f32[4096,2048]{1,0:T(8,128)} %fusion.83, f32[4096,2048]{1,0:T(8,128)} %fusion.81, f32[4096,2048]{1,0:T(8,128)} %fusion.82, bf16[4096,1024]{1,0:T(8,128)(2,1)} %get-tuple-element.433, bf16[2048,1024]{1,0:T(8,128)(2,1)} %all-gather.19.cloned.1.call-done), kind=kOutput, calls=%fused_computation.57 | convolution fusion | flops 17205035008 | bytes 146800640 | tf_op jit(solution)/shard_map/rf,df->rd/dot_general | solution.py:223
  1099.7 34.0 %convolution_add_fusion = f32[4096,2048]{1,0:T(8,128)} fusion(f32[4096,2048]{1,0:T(8,128)} %fusion.79, bf16[1024,2048]{1,0:T(8,128)(2,1)S(1)} %copy-done.42, f32[4096,1024]{1,0:T(8,128)} %fusion.80, f32[1024]{0:T(1024)S(1)} %copy-done.40), kind=kOutput, calls=%fused_computation.60 | convolution fusion | flops 17230200832 | bytes 88084480 | tf_op jit(solution)/shard_map/dot_general | solution.py:128
  1179.9 24.2 %fusion.88 = f32[2048,1024]{1,0:T(8,128)} fusion(bf16[4096,2048]{1,0:T(8,128)(2,1)} %all-gather.9.cloned.1.call-done, bf16[4096,1024]{1,0:T(8,128)(2,1)} %get-tuple-element.433), kind=kOutput, calls=%fused_computation.144 | convolution fusion | flops 17179869184 | bytes 33554432 | tf_op jit(solution)/shard_map/rd,rf->df/dot_general | solution.py:218
  1204.2 28.9 %fusion.76 = f32[1024,2048]{1,0:T(8,128)} fusion(bf16[4096,2048]{1,0:T(8,128)(2,1)} %all-gather.23.cloned.1.call-done, f32[4096,1024]{1,0:T(8,128)} %fusion.80, f32[1024]{0:T(1024)S(1)} %copy-done.40), kind=kOutput, calls=%fused_computation.133 | convolution fusion | flops 17221812224 | bytes 41947136 | tf_op jit(solution)/shard_map/rf,rd->fd/dot_general | solution.py:147
  1246.9 158.2 %reduce-scatter.11.cloned.1.call-done = f32[512,2048]{1,0:T(8,128)} async-done(((f32[4096,2048]{1,0:T(8,128)}), f32[512,2048]{1,0:T(8,128)}) %reduce-scatter.11.cloned.1.call-update) | async-done | bytes 4194320 | tf_op jit(solution)/shard_map/reduce_scatter | solution.py:219
  1410.6 320.8 %reduce-scatter.9.cloned.1.call-done = f32[512,2048]{1,0:T(8,128)} async-done(((f32[4096,2048]{1,0:T(8,128)}), f32[512,2048]{1,0:T(8,128)}) %reduce-scatter.9.cloned.1.call-update) | async-done | bytes 4194320 | tf_op jit(solution)/shard_map/reduce_scatter | solution.py:126
  1739.0 38.3 %all-reduce = (f32[2048]{0:T(1024)}, f32[2048]{0:T(1024)}, f32[2048]{0:T(1024)S(1)}) all-reduce(f32[2048]{0:T(1024)S(1)} %get-tuple-element.359, f32[2048]{0:T(1024)S(1)} %get-tuple-element.361, f32[2048]{0:T(1024)S(1)} %get-tuple-element.458), channel_id=1, replica_groups=mesh['dp'=4,'tensor'=8] {'dp','tensor'}, use_global_device_ids=true, to_apply=%region_16.17 | all-reduce | flops 6144 | bytes 49152 | tf_op jit(solution)/shard_map/psum | solution.py:232
  1777.3 30.9 %reduce-scatter.17.cloned.1.call-done = f32[512,256]{1,0:T(8,128)} async-done(((f32[2048,256]{1,0:T(8,128)}), f32[512,256]{1,0:T(8,128)}) %reduce-scatter.17.cloned.1.call-update) | async-done | bytes 524304 | tf_op jit(solution)/shard_map/reduce_scatter | solution.py:254
  1808.2 38.7 %reduce-scatter.15.cloned.1.call-done = f32[512,256]{1,0:T(8,128)} async-done(((f32[2048,256]{1,0:T(8,128)}), f32[512,256]{1,0:T(8,128)}) %reduce-scatter.15.cloned.1.call-update) | async-done | bytes 524304 | tf_op jit(solution)/shard_map/reduce_scatter | solution.py:253
  1847.0 38.9 %reduce-scatter.13.cloned.1.call-done = f32[512,256]{1,0:T(8,128)} async-done(((f32[2048,256]{1,0:T(8,128)}), f32[512,256]{1,0:T(8,128)}) %reduce-scatter.13.cloned.1.call-update) | async-done | bytes 524304 | tf_op jit(solution)/shard_map/reduce_scatter | solution.py:252
  1885.9 89.9 %reduce-scatter.21.cloned.1.call-done = f32[512,1024]{1,0:T(8,128)} async-done(((f32[2048,1024]{1,0:T(8,128)}), f32[512,1024]{1,0:T(8,128)}) %reduce-scatter.21.cloned.1.call-update) | async-done | bytes 2097168 | tf_op jit(solution)/shard_map/reduce_scatter | solution.py:255
  1975.8 90.2 %reduce-scatter.23.cloned.1.call-done = f32[1024,512]{1,0:T(8,128)} async-done(((f32[1024,2048]{1,0:T(8,128)}), f32[1024,512]{1,0:T(8,128)}) %reduce-scatter.23.cloned.1.call-update) | async-done | bytes 2097168 | tf_op jit(solution)/shard_map/reduce_scatter | solution.py:257
  (468 shorter events, 662.8 us)
Async XLA Ops:
  7.2 32.0 %all-gather.15.cloned.1.call-start = ((), (), s32[]{:S(2)}) async-start(), calls=%async_computation.11 | async-start | bytes 1310720 | tf_op jit(solution)/shard_map/all_gather | solution.py:81
  7.9 184.6 %all-gather.9.cloned.1.call-start = ((), (), s32[]{:S(2)}) async-start(), calls=%async_computation.8 | async-start | bytes 18874368 | tf_op jit(solution)/shard_map/all_gather | solution.py:87
  17.0 205.3 %all-gather.13.cloned.1.call-start = ((), (), s32[]{:S(2)}) async-start(), calls=%async_computation.10 | async-start | bytes 1310720 | tf_op jit(solution)/shard_map/all_gather | solution.py:80
  17.7 234.8 %all-gather.11.cloned.1.call-start = ((), (), s32[]{:S(2)}) async-start(), calls=%async_computation.9 | async-start | bytes 1310720 | tf_op jit(solution)/shard_map/all_gather | solution.py:82
  18.3 260.3 %all-gather.17.cloned.1.call-start = ((), (), s32[]{:S(2)}) async-start(), calls=%async_computation.12 | async-start | bytes 1310720 | tf_op jit(solution)/shard_map/all_gather | solution.py:84
  18.9 409.6 %all-gather.23.cloned.1.call-start = ((), (), s32[]{:S(2)}) async-start(), calls=%async_computation.16 | async-start | bytes 18874368 | tf_op jit(solution)/shard_map/all_gather | solution.py:145
  19.4 953.3 %all-gather.19.cloned.1.call-start = ((), (), s32[]{:S(2)}) async-start(), calls=%async_computation.13 | async-start | bytes 5242880 | tf_op jit(solution)/shard_map/all_gather | solution.py:83
  20.2 976.0 %all-gather.21.cloned.1.call-start = ((), (), s32[]{:S(2)}) async-start(), calls=%async_computation.14 | async-start | bytes 5242880 | tf_op jit(solution)/shard_map/all_gather | solution.py:85
  20.9 1384.2 %reduce-scatter.11.cloned.1.call-start = ((), (), s32[]{:S(2)}) async-start(), calls=%async_computation.17 | async-start | bytes 37748736 | tf_op jit(solution)/shard_map/reduce_scatter | solution.py:219
  22.7 432.1 %copy-start.20 = (f32[1024,32]{0,1:T(8,128)}, f32[1024,32]{0,1:T(8,128)S(1)}, u32[]{:S(2)}) copy-start(f32[1024,32]{0,1:T(8,128)S(1)} %get-tuple-element.467) | copy-start | bytes 393220
  972.8 23.4 %copy-start.40 = (f32[1024]{0:T(1024)S(1)}, f32[1024]{0:T(1024)}, u32[]{:S(2)}) copy-start(f32[1024]{0:T(1024)} %convert_element_type.123) | copy-start | bytes 12292
  1081.3 650.1 %reduce-scatter.9.cloned.1.call-start = ((), (), s32[]{:S(2)}) async-start(), calls=%async_computation.15 | async-start | bytes 37748736 | tf_op jit(solution)/shard_map/reduce_scatter | solution.py:126
  1133.7 643.6 %reduce-scatter.19.cloned.1.call-start = ((), (), s32[]{:S(2)}) async-start(), calls=%async_computation.21 | async-start | bytes 2621440 | tf_op jit(solution)/shard_map/reduce_scatter | solution.py:256
  1146.3 661.9 %reduce-scatter.17.cloned.1.call-start = ((), (), s32[]{:S(2)}) async-start(), calls=%async_computation.20 | async-start | bytes 2621440 | tf_op jit(solution)/shard_map/reduce_scatter | solution.py:254
  1156.6 690.4 %reduce-scatter.15.cloned.1.call-start = ((), (), s32[]{:S(2)}) async-start(), calls=%async_computation.19 | async-start | bytes 2621440 | tf_op jit(solution)/shard_map/reduce_scatter | solution.py:253
  1169.7 716.2 %reduce-scatter.13.cloned.1.call-start = ((), (), s32[]{:S(2)}) async-start(), calls=%async_computation.18 | async-start | bytes 2621440 | tf_op jit(solution)/shard_map/reduce_scatter | solution.py:252
  1179.7 796.2 %reduce-scatter.21.cloned.1.call-start = ((), (), s32[]{:S(2)}) async-start(), calls=%async_computation.22 | async-start | bytes 10485760 | tf_op jit(solution)/shard_map/reduce_scatter | solution.py:255
  1204.2 861.9 %reduce-scatter.23.cloned.1.call-start = ((), (), s32[]{:S(2)}) async-start(), calls=%async_computation.23 | async-start | bytes 10485760 | tf_op jit(solution)/shard_map/reduce_scatter | solution.py:257
  1233.1 172.1 %copy-start.2 = (bf16[512,2048]{1,0:T(8,128)(2,1)S(1)}, bf16[512,2048]{1,0:T(8,128)(2,1)}, u32[]{:S(2)}) copy-start(bf16[512,2048]{1,0:T(8,128)(2,1)} %param.23) | copy-start | bytes 6291460
  1233.1 172.0 %copy-start.26 = (f32[2048]{0:T(1024)S(1)}, f32[2048]{0:T(1024)}, u32[]{:S(2)}) copy-start(f32[2048]{0:T(1024)} %copy-done.25) | copy-start | bytes 24580
  1233.1 172.0 %copy-start.29 = (f32[512]{0:T(512)S(1)}, f32[512]{0:T(512)}, u32[]{:S(2)}) copy-start(f32[512]{0:T(512)} %copy-done.28) | copy-start | bytes 6148
  1233.8 174.7 %copy-start.33 = (f32[512]{0:T(512)S(1)}, f32[512]{0:T(512)}, u32[]{:S(2)}) copy-start(f32[512]{0:T(512)} %copy-done.32) | copy-start | bytes 6148
  1233.8 174.7 %copy-start.31 = (f32[512]{0:T(512)S(1)}, f32[512]{0:T(512)}, u32[]{:S(2)}) copy-start(f32[512]{0:T(512)} %copy-done.30) | copy-start | bytes 6148
  1777.3 289.3 %copy-start.36 = (f32[2048]{0:T(1024)}, f32[2048]{0:T(1024)S(1)}, u32[]{:S(2)}) copy-start(f32[2048]{0:T(1024)S(1)} %get-tuple-element.893) | copy-start | bytes 24580
  (69 other events, 317.5 us)
Sparse Core Ops, SparseCore 0:
  9.9 29.3 all-gather.14
  41.4 151.0 all-gather.8
  194.4 24.8 all-gather.12
  221.0 26.6 all-gather.10
  249.3 26.4 all-gather.16
  277.3 151.1 all-gather.22
  430.3 50.9 all-gather.18
  483.1 52.5 all-gather.20
  1081.4 323.6 reduce-scatter.10
  1407.5 323.8 reduce-scatter.8
  1735.0 34.3 reduce-scatter.18
  1773.0 35.1 reduce-scatter.16
  1811.8 35.1 reduce-scatter.14
  1850.7 35.2 reduce-scatter.12
  1889.4 86.3 reduce-scatter.20
  1979.6 86.3 reduce-scatter.22
where the time goes:
time: 2090 us; the launch traced here: 2070 us
  waiting for transfers between devices  1090 us (52%)
  matrix products  473 us (23%)
  local copies, waits for them, and re-layouts  297 us (14%)
  other arithmetic  95.4 us (5%)
  loops' own time  51.3 us (2%)
  blocking collectives  49.1 us (2%)
    reduce_scatter x1, waiting for transfers between devices, per_device(): lax.psum_scatter(jnp.dot(attended_low, full_out, preferred_element_type=j...  321 us
    dynamic_update_slice x20, local copies, waits for them, and re-layouts, per_device(): lax.map(backward_sequence, jnp.arange(seq_count))  181 us
    reduce_scatter x1, waiting for transfers between devices, per_device(): lax.psum_scatter(jnp.einsum('rk,dk->rd', query_grad, back_query, preferre...  158 us
    all_gather x1, waiting for transfers between devices, per_device(): group_rows = lax.all_gather(normed, 'tensor', axis=0, tiled=True)  153 us
    all_gather x1, waiting for transfers between devices, per_device(): upstream = lax.all_gather(grad_out, 'tensor', axis=0, tiled=True)  150 us
    reduce_scatter x1, waiting for transfers between devices, per_device(): lax.psum_scatter(down_wgrad, 'dp', scatter_dimension=1, tiled=True)  90.2 us
    reduce_scatter x1, waiting for transfers between devices, per_device(): lax.psum_scatter(up_wgrad, 'dp', scatter_dimension=0, tiled=True)  89.9 us
    dot_general x4, matrix products, project(): jnp.dot(group_rows, weight_part, preferred_element_type=jnp.float32)  60.7 us
  transfers between devices with their start and end apart: 16, of which 10 were waited for; matrix products, arithmetic and copies ran while one was open for 37% of the time, Pallas kernels for 0%

commit v1 on v0

--- a/solution.py
+++ b/solution.py
@@ -6,6 +6,17 @@
 HEAD_DIM = 64
 ROT = 32
 eps_norm = 1e-05
+
+
+def gather_by_hops(x, axis, dim):
+    peers = lax.axis_size(axis)
+    forward = [(i, (i + 1) % peers) for i in range(peers)]
+    parts = [x]
+    for hop in range(1, peers):
+        parts = [lax.ppermute(parts[0], axis, forward), *parts]
+    whole = jnp.concatenate(parts, axis=dim)
+    turn = (lax.axis_index(axis) + 1) * parts[-1].shape[dim]
+    return jnp.roll(whole, turn, axis=dim)
 
 
 def normalize(values, gain_in, shift_in):
@@ -84,7 +95,7 @@
         lax.all_gather(out_weight, "dp", axis=1, tiled=True),
         lax.all_gather(down_weight, "dp", axis=1, tiled=True),
     )
-    group_rows = lax.all_gather(normed, "tensor", axis=0, tiled=True)
+    group_rows = gather_by_hops(normed, "tensor", 0)
     cos_table, sin_table = rotary_tables(length, ROT)
 
     def project(weight_part, bias_part):

time: 2090 us -> 2020 us (0.967)
  waiting for transfers between devices: 1090 us -> 995 us
  local copies, waits for them, and re-layouts: 297 us -> 333 us
    ppermute x0 -> x7, waiting for transfers between devices: none -> 225 us  [gather_by_hops(): parts = [lax.ppermute(parts[0], axis, forward), *parts]]
    all_gather x1, waiting for transfers between devices: 153 us -> 0.02 us  [per_device(): back_rows = lax.all_gather(normed, 'tensor', axis=0, tiled=True)]
    all_gather x1, waiting for transfers between devices: 150 us -> 0.01 us  [per_device(): upstream = lax.all_gather(grad_out, 'tensor', axis=0, tiled=True)]
    unnamed x87 -> x119, local copies, waits for them, and re-layouts: 12.6 us -> 49.5 us
    reduce_scatter x1, waiting for transfers between devices: 30.9 us -> 0.02 us  [per_device(): lax.psum_scatter(value_wgrad, 'dp', scatter_dimension=0, tiled=True)]
    reduce_scatter x1, waiting for transfers between devices: 0.02 us -> 30.9 us  [per_device(): lax.psum_scatter(out_wgrad, 'dp', scatter_dimension=1, tiled=True)]
  transfers between devices with their start and end apart: 16 -> 23, of which waited for: 10 -> 14; matrix products, arithmetic and copies ran while one was open for 37% -> 44% of each run, Pallas kernels for 0% -> 0%
where the time goes in v1:
time: 2020 us; the launch traced here: 2010 us
  waiting for transfers between devices  995 us (49%)
  matrix products  472 us (23%)
  local copies, waits for them, and re-layouts  333 us (16%)
  other arithmetic  91.9 us (5%)
  loops' own time  51.6 us (3%)
  blocking collectives  50.7 us (3%)
    reduce_scatter x1, waiting for transfers between devices, per_device(): lax.psum_scatter(jnp.dot(attended_low, full_out, preferred_element_type=j...  321 us
    ppermute x7, waiting for transfers between devices, gather_by_hops(): parts = [lax.ppermute(parts[0], axis, forward), *parts]  225 us
    dynamic_update_slice x20, local copies, waits for them, and re-layouts, per_device(): lax.map(backward_sequence, jnp.arange(seq_count))  181 us
    reduce_scatter x1, waiting for transfers between devices, per_device(): lax.psum_scatter(jnp.einsum('rk,dk->rd', query_grad, back_query, preferre...  157 us
    reduce_scatter x1, waiting for transfers between devices, per_device(): lax.psum_scatter(down_wgrad, 'dp', scatter_dimension=1, tiled=True)  90.2 us
    reduce_scatter x1, waiting for transfers between devices, per_device(): lax.psum_scatter(up_wgrad, 'dp', scatter_dimension=0, tiled=True)  89.9 us
    dot_general x4, matrix products, project(): jnp.dot(group_rows, weight_part, preferred_element_type=jnp.float32)  61.5 us
    unnamed x119, local copies, waits for them, and re-layouts  49.5 us
  transfers between devices with their start and end apart: 23, of which 14 were waited for; matrix products, arithmetic and copies ran while one was open for 44% of the time, Pallas kernels for 0%

profile of v1, /device:TPU:0, one launch (start us, length us, event | category | flops | bytes accessed | tf_op | source)
XLA Modules:
  0.0 2011.1 jit_solution(7647000457288992646)
XLA Ops:
  15.0 28.0 %collective-permute-done = bf16[512,2048]{1,0:T(8,128)(2,1)S(1)} collective-permute-done((bf16[512,2048]{1,0:T(8,128)(2,1)}, bf16[512,2048]{1,0:T(8,128)(2,1)S(1)}, u32[]{:S(2)}, u32[]{:S(2)}) %collective-permute-start) | collective-permute-done | bytes 2097184 | tf_op jit(solution)/shard_map/ppermute | solution.py:16
  72.9 27.4 %collective-permute-done.2 = bf16[512,2048]{1,0:T(8,128)(2,1)} collective-permute-done((bf16[512,2048]{1,0:T(8,128)(2,1)S(1)}, bf16[512,2048]{1,0:T(8,128)(2,1)}, u32[]{:S(2)}, u32[]{:S(2)}) %collective-permute-start.2) | collective-permute-done | bytes 2097184 | tf_op jit(solution)/shard_map/ppermute | solution.py:16
  100.4 27.5 %collective-permute-done.3 = bf16[512,2048]{1,0:T(8,128)(2,1)} collective-permute-done((bf16[512,2048]{1,0:T(8,128)(2,1)}, bf16[512,2048]{1,0:T(8,128)(2,1)}, u32[]{:S(2)}, u32[]{:S(2)}) %collective-permute-start.3) | collective-permute-done | bytes 2097184 | tf_op jit(solution)/shard_map/ppermute | solution.py:16
  127.9 27.5 %collective-permute-done.4 = bf16[512,2048]{1,0:T(8,128)(2,1)S(1)} collective-permute-done((bf16[512,2048]{1,0:T(8,128)(2,1)}, bf16[512,2048]{1,0:T(8,128)(2,1)S(1)}, u32[]{:S(2)}, u32[]{:S(2)}) %collective-permute-start.4) | collective-permute-done | bytes 2097184 | tf_op jit(solution)/shard_map/ppermute | solution.py:16
  156.7 27.4 %collective-permute-done.5 = bf16[512,2048]{1,0:T(8,128)(2,1)} collective-permute-done((bf16[512,2048]{1,0:T(8,128)(2,1)S(1)}, bf16[512,2048]{1,0:T(8,128)(2,1)}, u32[]{:S(2)}, u32[]{:S(2)}) %collective-permute-start.5) | collective-permute-done | bytes 2097184 | tf_op jit(solution)/shard_map/ppermute | solution.py:16
  186.1 59.8 %collective-permute-done.6 = bf16[512,2048]{1,0:T(8,128)(2,1)} collective-permute-done((bf16[512,2048]{1,0:T(8,128)(2,1)}, bf16[512,2048]{1,0:T(8,128)(2,1)}, u32[]{:S(2)}, u32[]{:S(2)}) %collective-permute-start.6) | collective-permute-done | bytes 2097184 | tf_op jit(solution)/shard_map/ppermute | solution.py:16
  382.4 103.1 %while.44 = (s32[]{:T(128)}, bf16[8,512,4,64]{1,3,2,0:T(8,128)(2,1)S(1)}, f32[8,4,512]{2,1,0:T(4,128)S(1)}, s32[8]{0:T(128)S(1)}, bf16[4,1024,4,64]{1,3,2,0:T(8,...) while((s32[]{:T(128)}, ...), condition=%wide.region_5.6_spmd, body=%wide.region_2.5_spmd.sunk | while | flops 562558976 | bytes 29182452 | solution.py:133
  530.8 343.6 %while.46 = (s32[]{:T(128)}, f32[4,1024,4,64]{1,0,3,2:T(4,128)}, f32[4,1024,4,64]{1,0,3,2:T(4,128)}, bf16[4,1024,4,64]{1,3,2,0:T(8,128)(2,1)}, s32[4]{0:T(128)S(...) while((s32[]{:T(128)}, f32[4,1024,4,64]{1,0,3,2:T(4,128)}, ...), condition=%wide.region_11.12_spmd, body=%wide.region_7.11_spmd.sunk | while | flops 1375598592 | bytes 110209856 | solution.py:214
  536.4 33.4 %while.47 = (s32[]{:T(128)}, f32[1024,4,64]{0,2,1:T(8,128)S(1)}, f32[1024,4,64]{0,2,1:T(8,128)}, f32[2,512,4,64]{1,3,2,0:T(8,128)}, s32[2]{0:T(128)S(1)}, /*inde...) while((s32[]{:T(128)}, f32[1024,4,64]{0,2,1:T(8,128)S(1)}, ...), condition=%wide.region_10.10_spmd.clone, body=%wide.region_8.9_spmd.clone.sunk | while | flops 1375598592 | bytes 89196952 | solution.py:209
  622.2 33.4 %while.47 = (s32[]{:T(128)}, f32[1024,4,64]{0,2,1:T(8,128)S(1)}, f32[1024,4,64]{0,2,1:T(8,128)}, f32[2,512,4,64]{1,3,2,0:T(8,128)}, s32[2]{0:T(128)S(1)}, /*inde...) while((s32[]{:T(128)}, f32[1024,4,64]{0,2,1:T(8,128)S(1)}, ...), condition=%wide.region_10.10_spmd.clone, body=%wide.region_8.9_spmd.clone.sunk | while | flops 1375598592 | bytes 89196952 | solution.py:209
  707.9 33.4 %while.47 = (s32[]{:T(128)}, f32[1024,4,64]{0,2,1:T(8,128)S(1)}, f32[1024,4,64]{0,2,1:T(8,128)}, f32[2,512,4,64]{1,3,2,0:T(8,128)}, s32[2]{0:T(128)S(1)}, /*inde...) while((s32[]{:T(128)}, f32[1024,4,64]{0,2,1:T(8,128)S(1)}, ...), condition=%wide.region_10.10_spmd.clone, body=%wide.region_8.9_spmd.clone.sunk | while | flops 1375598592 | bytes 89196952 | solution.py:209
  793.7 33.4 %while.47 = (s32[]{:T(128)}, f32[1024,4,64]{0,2,1:T(8,128)S(1)}, f32[1024,4,64]{0,2,1:T(8,128)}, f32[2,512,4,64]{1,3,2,0:T(8,128)}, s32[2]{0:T(128)S(1)}, /*inde...) while((s32[]{:T(128)}, f32[1024,4,64]{0,2,1:T(8,128)S(1)}, ...), condition=%wide.region_10.10_spmd.clone, body=%wide.region_8.9_spmd.clone.sunk | while | flops 1375598592 | bytes 89196952 | solution.py:209
  932.4 36.3 %convert_reduce_fusion = (f32[1024]{0:T(1024)}, bf16[4096,1024]{1,0:T(8,128)(2,1)}) fusion(f32[4096,1024]{1,0:T(8,128)} %fusion.49, f32[1024]{0:T(1024)S(1)} %copy-done.49, bf16[4096,2048]{1,0:T(8,128)(2,1)} %all-gather.21.cloned.1.call-done, bf16[1024,2048]{1,0:T(8,128)(2,1)} %all-gather.19.cloned.1.call-done), kind=kOutput, calls=%fused_computation.68 | convolution fusion | flops 17276338176 | bytes 46145536 | tf_op jit(solution)/shard_map/rd,fd->rf/dot_general | solution.py:162
  968.7 48.6 %add_add_fusion = f32[4096,2048]{1,0:T(8,128)} fusion(f32[4096,2048]{1,0:T(8,128)} %fusion.105, f32[4096,2048]{1,0:T(8,128)} %fusion.103, f32[4096,2048]{1,0:T(8,128)} %fusion.104, bf16[4096,1024]{1,0:T(8,128)(2,1)} %get-tuple-element.433, bf16[2048,1024]{1,0:T(8,128)(2,1)} %all-gather.17.cloned.1.call-done), kind=kOutput, calls=%fused_computation.57 | convolution fusion | flops 17205035008 | bytes 146800640 | tf_op jit(solution)/shard_map/rf,df->rd/dot_general | solution.py:234
  1035.7 34.1 %convolution_add_fusion = f32[4096,2048]{1,0:T(8,128)} fusion(f32[4096,2048]{1,0:T(8,128)} %fusion.102, bf16[1024,2048]{1,0:T(8,128)(2,1)S(1)} %copy-done.51, f32[4096,1024]{1,0:T(8,128)} %fusion.49, f32[1024]{0:T(1024)S(1)} %copy-done.49), kind=kOutput, calls=%fused_computation.60 | convolution fusion | flops 17230200832 | bytes 88084480 | tf_op jit(solution)/shard_map/dot_general | solution.py:139
  1141.6 28.8 %fusion.99 = f32[1024,2048]{1,0:T(8,128)} fusion(bf16[4096,2048]{1,0:T(8,128)(2,1)} %all-gather.21.cloned.1.call-done, f32[4096,1024]{1,0:T(8,128)} %fusion.49, f32[1024]{0:T(1024)S(1)} %copy-done.49), kind=kOutput, calls=%fused_computation.161 | convolution fusion | flops 17221812224 | bytes 41947136 | tf_op jit(solution)/shard_map/rf,rd->fd/dot_general | solution.py:158
  1185.8 156.8 %reduce-scatter.11.cloned.1.call-done = f32[512,2048]{1,0:T(8,128)} async-done(((f32[4096,2048]{1,0:T(8,128)}), f32[512,2048]{1,0:T(8,128)}) %reduce-scatter.11.cloned.1.call-update) | async-done | bytes 4194320 | tf_op jit(solution)/shard_map/reduce_scatter | solution.py:230
  1348.1 320.8 %reduce-scatter.9.cloned.1.call-done = f32[512,2048]{1,0:T(8,128)} async-done(((f32[4096,2048]{1,0:T(8,128)}), f32[512,2048]{1,0:T(8,128)}) %reduce-scatter.9.cloned.1.call-update) | async-done | bytes 4194320 | tf_op jit(solution)/shard_map/reduce_scatter | solution.py:137
  1676.4 38.4 %all-reduce = (f32[2048]{0:T(1024)}, f32[2048]{0:T(1024)}, f32[2048]{0:T(1024)S(1)}) all-reduce(f32[2048]{0:T(1024)S(1)} %get-tuple-element.359, f32[2048]{0:T(1024)S(1)} %get-tuple-element.361, f32[2048]{0:T(1024)S(1)} %get-tuple-element.458), channel_id=1, replica_groups=mesh['dp'=4,'tensor'=8] {'dp','tensor'}, use_global_device_ids=true, to_apply=%region_16.17 | all-reduce | flops 6144 | bytes 49152 | tf_op jit(solution)/shard_map/psum | solution.py:243
  1714.8 30.9 %reduce-scatter.19.cloned.1.call-done = f32[256,512]{1,0:T(8,128)} async-done(((f32[256,2048]{1,0:T(8,128)}), f32[256,512]{1,0:T(8,128)}) %reduce-scatter.19.cloned.1.call-update) | async-done | bytes 524304 | tf_op jit(solution)/shard_map/reduce_scatter | solution.py:267
  1745.7 38.8 %reduce-scatter.15.cloned.1.call-done = f32[512,256]{1,0:T(8,128)} async-done(((f32[2048,256]{1,0:T(8,128)}), f32[512,256]{1,0:T(8,128)}) %reduce-scatter.15.cloned.1.call-update) | async-done | bytes 524304 | tf_op jit(solution)/shard_map/reduce_scatter | solution.py:264
  1784.4 38.9 %reduce-scatter.13.cloned.1.call-done = f32[512,256]{1,0:T(8,128)} async-done(((f32[2048,256]{1,0:T(8,128)}), f32[512,256]{1,0:T(8,128)}) %reduce-scatter.13.cloned.1.call-update) | async-done | bytes 524304 | tf_op jit(solution)/shard_map/reduce_scatter | solution.py:263
  1823.3 89.9 %reduce-scatter.21.cloned.1.call-done = f32[512,1024]{1,0:T(8,128)} async-done(((f32[2048,1024]{1,0:T(8,128)}), f32[512,1024]{1,0:T(8,128)}) %reduce-scatter.21.cloned.1.call-update) | async-done | bytes 2097168 | tf_op jit(solution)/shard_map/reduce_scatter | solution.py:266
  1913.3 90.2 %reduce-scatter.23.cloned.1.call-done = f32[1024,512]{1,0:T(8,128)} async-done(((f32[1024,2048]{1,0:T(8,128)}), f32[1024,512]{1,0:T(8,128)}) %reduce-scatter.23.cloned.1.call-update) | async-done | bytes 2097168 | tf_op jit(solution)/shard_map/reduce_scatter | solution.py:268
  (516 shorter events, 794.3 us)
Async XLA Ops:
  7.2 277.9 %all-gather.11.cloned.1.call-start = ((), (), s32[]{:S(2)}) async-start(), calls=%async_computation.9 | async-start | bytes 1310720 | tf_op jit(solution)/shard_map/all_gather | solution.py:91
  7.9 307.1 %all-gather.13.cloned.1.call-start = ((), (), s32[]{:S(2)}) async-start(), calls=%async_computation.10 | async-start | bytes 1310720 | tf_op jit(solution)/shard_map/all_gather | solution.py:92
  8.7 336.9 %all-gather.9.cloned.1.call-start = ((), (), s32[]{:S(2)}) async-start(), calls=%async_computation.8 | async-start | bytes 1310720 | tf_op jit(solution)/shard_map/all_gather | solution.py:93
  9.4 476.1 %all-gather.17.cloned.1.call-start = ((), (), s32[]{:S(2)}) async-start(), calls=%async_computation.12 | async-start | bytes 5242880 | tf_op jit(solution)/shard_map/all_gather | solution.py:94
  10.0 499.7 %all-gather.15.cloned.1.call-start = ((), (), s32[]{:S(2)}) async-start(), calls=%async_computation.11 | async-start | bytes 1310720 | tf_op jit(solution)/shard_map/all_gather | solution.py:95
  10.6 499.1 %all-gather.21.cloned.1.call-start = ((), (), s32[]{:S(2)}) async-start(), calls=%async_computation.15 | async-start | bytes 18874368 | tf_op jit(solution)/shard_map/all_gather | solution.py:156
  11.2 921.2 %all-gather.19.cloned.1.call-start = ((), (), s32[]{:S(2)}) async-start(), calls=%async_computation.13 | async-start | bytes 5242880 | tf_op jit(solution)/shard_map/all_gather | solution.py:96
  14.6 28.4 %collective-permute-start = (bf16[512,2048]{1,0:T(8,128)(2,1)}, bf16[512,2048]{1,0:T(8,128)(2,1)S(1)}, u32[]{:S(2)}, u32[]{:S(2)}) collective-permute-start(bf16[512,2048]{1,0:T(8,128)(2,1)} %fusion.76), channel_id=1, source_target_pairs={{0,1},{1,2},{2,3},{3,4},{4,5},{5,6},{6,7},{7,0},{8,9},{9,10},{10,1... | collective-permute-start | bytes 6291464 | tf_op jit(solution)/shard_map/ppermute | solution.py:16
  44.4 27.3 %collective-permute-start.1 = (bf16[512,2048]{1,0:T(8,128)(2,1)S(1)}, bf16[512,2048]{1,0:T(8,128)(2,1)S(1)}, u32[]{:S(2)}, u32[]{:S(2)}) collective-permute-start(bf16[512,2048]{1,0:T(8,128)(2,1)S(1)} %collective-permute-done), channel_id=1, source_target_pairs={{0,1},{1,2},{2,3},{3,4},{4,5},{5,6},{6,7},{7,0},{8,9},{9,10},{10,1... | collective-permute-start | bytes 6291464 | tf_op jit(solution)/shard_map/ppermute | solution.py:16
  72.9 27.4 %collective-permute-start.2 = (bf16[512,2048]{1,0:T(8,128)(2,1)S(1)}, bf16[512,2048]{1,0:T(8,128)(2,1)}, u32[]{:S(2)}, u32[]{:S(2)}) collective-permute-start(bf16[512,2048]{1,0:T(8,128)(2,1)S(1)} %collective-permute-done.1), channel_id=1, source_target_pairs={{0,1},{1,2},{2,3},{3,4},{4,5},{5,6},{6,7},{7,0},{8,9},{9,10},{10,1... | collective-permute-start | bytes 6291464 | tf_op jit(solution)/shard_map/ppermute | solution.py:16
  100.3 27.6 %collective-permute-start.3 = (bf16[512,2048]{1,0:T(8,128)(2,1)}, bf16[512,2048]{1,0:T(8,128)(2,1)}, u32[]{:S(2)}, u32[]{:S(2)}) collective-permute-start(bf16[512,2048]{1,0:T(8,128)(2,1)} %collective-permute-done.2), channel_id=1, source_target_pairs={{0,1},{1,2},{2,3},{3,4},{4,5},{5,6},{6,7},{7,0},{8,9},{9,10},{10,1... | collective-permute-start | bytes 6291464 | tf_op jit(solution)/shard_map/ppermute | solution.py:16
  100.3 969.6 %all-gather.23.cloned.1.call-start = ((), (), s32[]{:S(2)}) async-start(), calls=%async_computation.17 | async-start | bytes 18874368 | tf_op jit(solution)/shard_map/all_gather | solution.py:155
  127.9 27.5 %collective-permute-start.4 = (bf16[512,2048]{1,0:T(8,128)(2,1)}, bf16[512,2048]{1,0:T(8,128)(2,1)S(1)}, u32[]{:S(2)}, u32[]{:S(2)}) collective-permute-start(bf16[512,2048]{1,0:T(8,128)(2,1)} %collective-permute-done.3), channel_id=1, source_target_pairs={{0,1},{1,2},{2,3},{3,4},{4,5},{5,6},{6,7},{7,0},{8,9},{9,10},{10,1... | collective-permute-start | bytes 6291464 | tf_op jit(solution)/shard_map/ppermute | solution.py:16
  156.7 27.4 %collective-permute-start.5 = (bf16[512,2048]{1,0:T(8,128)(2,1)S(1)}, bf16[512,2048]{1,0:T(8,128)(2,1)}, u32[]{:S(2)}, u32[]{:S(2)}) collective-permute-start(bf16[512,2048]{1,0:T(8,128)(2,1)S(1)} %collective-permute-done.4), channel_id=1, source_target_pairs={{0,1},{1,2},{2,3},{3,4},{4,5},{5,6},{6,7},{7,0},{8,9},{9,10},{10,1... | collective-permute-start | bytes 6291464 | tf_op jit(solution)/shard_map/ppermute | solution.py:16
  184.0 61.8 %collective-permute-start.6 = (bf16[512,2048]{1,0:T(8,128)(2,1)}, bf16[512,2048]{1,0:T(8,128)(2,1)}, u32[]{:S(2)}, u32[]{:S(2)}) collective-permute-start(bf16[512,2048]{1,0:T(8,128)(2,1)} %collective-permute-done.5), channel_id=1, source_target_pairs={{0,1},{1,2},{2,3},{3,4},{4,5},{5,6},{6,7},{7,0},{8,9},{9,10},{10,1... | collective-permute-start | bytes 6291464 | tf_op jit(solution)/shard_map/ppermute | solution.py:16
  184.1 1158.6 %reduce-scatter.11.cloned.1.call-start = ((), (), s32[]{:S(2)}) async-start(), calls=%async_computation.16 | async-start | bytes 37748736 | tf_op jit(solution)/shard_map/reduce_scatter | solution.py:230
  1017.3 651.5 %reduce-scatter.9.cloned.1.call-start = ((), (), s32[]{:S(2)}) async-start(), calls=%async_computation.14 | async-start | bytes 37748736 | tf_op jit(solution)/shard_map/reduce_scatter | solution.py:137
  1069.8 645.0 %reduce-scatter.17.cloned.1.call-start = ((), (), s32[]{:S(2)}) async-start(), calls=%async_computation.20 | async-start | bytes 2621440 | tf_op jit(solution)/shard_map/reduce_scatter | solution.py:265
  1081.3 664.4 %reduce-scatter.19.cloned.1.call-start = ((), (), s32[]{:S(2)}) async-start(), calls=%async_computation.21 | async-start | bytes 2621440 | tf_op jit(solution)/shard_map/reduce_scatter | solution.py:267
  1094.0 690.5 %reduce-scatter.15.cloned.1.call-start = ((), (), s32[]{:S(2)}) async-start(), calls=%async_computation.19 | async-start | bytes 2621440 | tf_op jit(solution)/shard_map/reduce_scatter | solution.py:264
  1107.1 716.2 %reduce-scatter.13.cloned.1.call-start = ((), (), s32[]{:S(2)}) async-start(), calls=%async_computation.18 | async-start | bytes 2621440 | tf_op jit(solution)/shard_map/reduce_scatter | solution.py:263
  1117.0 796.2 %reduce-scatter.21.cloned.1.call-start = ((), (), s32[]{:S(2)}) async-start(), calls=%async_computation.22 | async-start | bytes 10485760 | tf_op jit(solution)/shard_map/reduce_scatter | solution.py:266
  1141.6 861.9 %reduce-scatter.23.cloned.1.call-start = ((), (), s32[]{:S(2)}) async-start(), calls=%async_computation.23 | async-start | bytes 10485760 | tf_op jit(solution)/shard_map/reduce_scatter | solution.py:268
  1714.8 289.3 %copy-start.43 = (f32[2048]{0:T(1024)}, f32[2048]{0:T(1024)S(1)}, u32[]{:S(2)}) copy-start(f32[2048]{0:T(1024)S(1)} %get-tuple-element.893) | copy-start | bytes 24580
  (85 other events, 3170.0 us)
Sparse Core Ops, SparseCore 0:
  9.9 29.3 all-gather.10
  41.1 26.6 all-gather.12
  69.6 26.6 all-gather.8
  98.0 52.6 all-gather.16
  152.4 26.4 all-gather.14
  180.3 168.1 all-gather.20
  350.3 51.3 all-gather.18
  403.9 151.0 all-gather.22
  1017.5 325.0 reduce-scatter.10
  1344.9 323.8 reduce-scatter.8
  1672.4 34.3 reduce-scatter.16
  1710.5 35.1 reduce-scatter.18
  1749.2 35.1 reduce-scatter.14
  1788.1 35.1 reduce-scatter.12
  1826.8 86.3 reduce-scatter.20
  1917.1 86.3 reduce-scatter.22
